TPU v7x, 256 devices: a whole 4x4x8 slice. The times are simulated.
256 devices in a mesh: space: 128 (over z, y, x), rep: 2 (over core).
Axes of the slice: x: 4, y: 4, z: 8, core: 2. Of those that a mesh axis runs over, the one named last changes fastest.
Arguments:
- features: bfloat16 [2, 512, 64, 512], P('rep', 'space'), may hold values from -6 to 6
- neighbours: int32 [2, 512, 26], P('rep', 'space'), may hold values from -1 to 35, as said below
- send_list: int32 [2, 128, 2, 16], P('rep', 'space'), may hold values from -1 to 3, as said below
- w_fine: bfloat16 [64, 1728], replicated, may hold values from -0.15625 to 0.15625
- w_down: bfloat16 [64, 512], replicated, may hold values from -0.25 to 0.25
- w_coarse: bfloat16 [64, 1728], replicated, may hold values from -0.15625 to 0.15625
- w_up: bfloat16 [64, 512], replicated, may hold values from -0.75 to 0.75
- cotangent: bfloat16 [2, 512, 64, 512], P('rep', 'space'), may hold values from -6 to 6
Outputs:
- decoded: bfloat16 [2, 512, 64, 512], P('rep', 'space')
- grad_fine: float32 [64, 1728], replicated
- grad_down: float32 [64, 512], replicated
- grad_coarse: float32 [64, 1728], replicated
- grad_up: float32 [64, 512], replicated
Inputs may be any that keep to these rules, and one draw needn't show every extreme that they name: `neighbours`: A scene is a corridor 4 block positions across in the second and third dimensions; device d holds the occupied positions whose first coordinate lies in 4 d .. 4 d + 3, in Morton order. Entries follow true adjacency: below 4 a block of the same device, 4 + s (s < 4**2) the block of device d - 1 in slot s of its side 0, 4 + 4**2 + s the block of device d + 1 in slot s of its side 1, -1 an empty or outside position. In every slab the positions (0, 3, 3) and (3, 3, 3) are occupied and (3, 0, 0) is empty. send_list[d, 0, y * 4 + z] is device d's block at the last first-coordinate plane of its slab and position (y, z), send_list[d, 1, y * 4 + z] the one at the first plane; -1 where that position is empty.
All inputs are finite; a program needn't handle non-finite values.
Results may differ from a plain program's by a relative error of at most 0.007.
Values may be sent and summed in bfloat16 or wider, within the bound.
No kernel may reach another device: no remote copies, remote signals or barrier semaphores. Data moves between devices by JAX's collectives and lax.ppermute only.
A program may use at most 128 MiB of HBM per device.

v0:
```python
import math
import jax
import jax.numpy as jnp
from jax import lax
from jax.sharding import PartitionSpec as P

EDGE = 8
DIRECTIONS = [
    (a, c, e) for a in (-1, 0, 1) for c in (-1, 0, 1) for e in (-1, 0, 1) if (a, c, e) != (0, 0, 0)
]


def passed_along(block, axis, distance):
    devices = range(lax.axis_size(axis))
    route = [(i - distance, i) for i in devices if i - distance in devices]
    return lax.ppermute(block, axis, route)


def silu_slope(values):
    sig = jax.nn.sigmoid(values)
    return sig * (1.0 + values * (1.0 - sig))


def source_range(step, side):
    if step < 0:
        return slice(side - 1, side)
    if step == 0:
        return slice(0, side)
    return slice(0, 1)


def target_range(step, side):
    if step < 0:
        return slice(0, 1)
    if step == 0:
        return slice(1, side + 1)
    return slice(side + 1, side + 2)


def assemble(own_blocks, combined, sources, side):
    count, channels = (own_blocks.shape[0], own_blocks.shape[1])
    cubes = combined.reshape(combined.shape[0], channels, side, side, side)
    padded = jnp.zeros((count, channels, side + 2, side + 2, side + 2), own_blocks.dtype)
    padded = padded.at[:, :, 1 : side + 1, 1 : side + 1, 1 : side + 1].set(
        own_blocks.reshape(count, channels, side, side, side)
    )
    for k, (a, c, e) in enumerate(DIRECTIONS):
        part_cells = cubes[
            :, :, source_range(a, side), source_range(c, side), source_range(e, side)
        ]
        source_ids = sources[:, k]
        gathered = jnp.take(part_cells, jnp.maximum(source_ids, 0), axis=0)
        gathered = jnp.where(
            (source_ids >= 0)[:, None, None, None, None], gathered, jnp.zeros_like(gathered)
        )
        padded = padded.at[
            :, :, target_range(a, side), target_range(c, side), target_range(e, side)
        ].set(gathered)
    return padded


def lattice_columns(padded, side):
    count, channels = (padded.shape[0], padded.shape[1])
    parts_list = [
        padded[:, :, a : a + side, c : c + side, e : e + side].reshape(count, channels, side**3)
        for a in range(3)
        for c in range(3)
        for e in range(3)
    ]
    return jnp.concatenate(parts_list, axis=1)


def spread_back(back_cols, side):
    count = back_cols.shape[0]
    channels = back_cols.shape[1] // 27
    result = jnp.zeros((count, channels, side + 2, side + 2, side + 2), jnp.float32)
    for a in range(3):
        for c in range(3):
            for e in range(3):
                offset = 9 * a + 3 * c + e
                piece = back_cols[:, offset * channels : (offset + 1) * channels].reshape(
                    count, channels, side, side, side
                )
                result = result.at[:, :, a : a + side, c : c + side, e : e + side].add(piece)
    return result


def to_patches(field, side):
    count, channels = (field.shape[0], field.shape[1])
    half = side // 2
    shaped = field.reshape(count, channels, half, 2, half, 2, half, 2).transpose(
        0, 3, 5, 7, 1, 2, 4, 6
    )
    return shaped.reshape(count, 8 * channels, half**3)


def from_patches(values, half):
    count = values.shape[0]
    channels = values.shape[1] // 8
    shaped = values.reshape(count, 2, 2, 2, channels, half, half, half).transpose(
        0, 4, 5, 1, 6, 2, 7, 3
    )
    return shaped.reshape(count, channels, 8 * half**3)


def shards(features, neighbours, send_list, w_fine, w_down, w_coarse, w_up, cotangent):
    f32 = jnp.float32
    fine_in = features[0]
    sources = neighbours[0]
    sends = send_list[0, 0]
    block_count, channels = (fine_in.shape[0], fine_in.shape[1])
    slot_count = sends.shape[1]
    peer_count = lax.axis_size("space")
    coarse_side = EDGE // 2
    upper_ids = jnp.maximum(sends[0], 0)
    lower_ids = jnp.maximum(sends[1], 0)
    to_upper = jnp.take(fine_in, upper_ids, axis=0)
    to_lower = jnp.take(fine_in, lower_ids, axis=0)
    arrived = []
    for offset, payload in ((1, to_upper), (-1, to_lower)):
        arrived.append(passed_along(payload, "space", offset))
    halo0 = assemble(fine_in, jnp.concatenate([fine_in] + arrived, axis=0), sources, EDGE)
    pad_groups = halo0.reshape((block_count // 4, 4) + halo0.shape[1:])

    def fine_forward(pad_group):
        return jnp.einsum(
            "ok,gkv->gov", w_fine, lattice_columns(pad_group, EDGE), preferred_element_type=f32
        )

    fine_pre = lax.map(fine_forward, pad_groups).reshape(block_count, channels, EDGE**3)
    hidden0 = jax.nn.silu(fine_pre).astype(jnp.bfloat16)
    patches0 = to_patches(hidden0, EDGE)
    coarse_pre = jnp.einsum("ok,bkv->bov", w_down, patches0, preferred_element_type=f32)
    hidden1 = jax.nn.silu(coarse_pre).astype(jnp.bfloat16)
    coarse_upper = jnp.take(hidden1, upper_ids, axis=0)
    coarse_lower = jnp.take(hidden1, lower_ids, axis=0)
    arrived1 = []
    for offset, payload in ((1, coarse_upper), (-1, coarse_lower)):
        arrived1.append(passed_along(payload, "space", offset))
    halo1 = assemble(hidden1, jnp.concatenate([hidden1] + arrived1, axis=0), sources, coarse_side)
    columns1 = lattice_columns(halo1, coarse_side)
    coarse_conv = jnp.einsum("ok,bkv->bov", w_coarse, columns1, preferred_element_type=f32)
    gated = jax.nn.silu(coarse_conv).astype(jnp.bfloat16)
    up_terms = from_patches(
        jnp.einsum("ik,biv->bkv", w_up, gated, preferred_element_type=f32), coarse_side
    )
    decoded = (hidden0.astype(f32) + up_terms).astype(jnp.bfloat16)
    cot_patch = to_patches(cotangent[0], EDGE)
    grad_up = jnp.einsum("biv,bkv->ik", gated, cot_patch, preferred_element_type=f32)
    up_back = jnp.einsum("ik,bkv->biv", w_up, cot_patch, preferred_element_type=f32)
    delta_up = (up_back * silu_slope(coarse_conv)).astype(jnp.bfloat16)
    grad_coarse = jnp.einsum("bov,bkv->ok", delta_up, columns1, preferred_element_type=f32)
    back_cols = jnp.einsum("ok,bov->bkv", w_coarse, delta_up, preferred_element_type=f32)
    back_pad = spread_back(back_cols, coarse_side)
    slot_total = block_count + 2 * slot_count
    slot_ids = jnp.arange(slot_total, dtype=jnp.int32)
    accumulated = jnp.zeros((slot_total, channels, coarse_side, coarse_side, coarse_side), f32)
    for k, (a, c, e) in enumerate(DIRECTIONS):
        piece = back_pad[
            :,
            :,
            target_range(a, coarse_side),
            target_range(c, coarse_side),
            target_range(e, coarse_side),
        ]
        selector = (sources[:, k][:, None] == slot_ids[None, :]).astype(f32)
        moved = jnp.einsum("bm,bcxyz->mcxyz", selector, piece, precision=lax.Precision.HIGHEST)
        accumulated = accumulated.at[
            :,
            :,
            source_range(a, coarse_side),
            source_range(c, coarse_side),
            source_range(e, coarse_side),
        ].add(moved)
    lower_owned = accumulated[block_count : block_count + slot_count][
        :, :, coarse_side - 1
    ].reshape(slot_count, channels * coarse_side**2)
    upper_owned = accumulated[block_count + slot_count :][:, :, 0].reshape(
        slot_count, channels * coarse_side**2
    )
    returned = []
    for offset, payload in ((-1, lower_owned), (1, upper_owned)):
        returned.append(
            passed_along(payload.astype(jnp.bfloat16), "space", offset).astype(payload.dtype)
        )
    block_ids = jnp.arange(block_count, dtype=jnp.int32)
    chooser_upper = (sends[0][:, None] == block_ids[None, :]).astype(f32)
    chooser_lower = (sends[1][:, None] == block_ids[None, :]).astype(f32)
    face_high = jnp.einsum("sb,sf->bf", chooser_upper, returned[0], precision=lax.Precision.HIGHEST)
    face_low = jnp.einsum("sb,sf->bf", chooser_lower, returned[1], precision=lax.Precision.HIGHEST)
    centre = back_pad[:, :, 1 : coarse_side + 1, 1 : coarse_side + 1, 1 : coarse_side + 1]
    grad_cube = centre + accumulated[:block_count]
    grad_cube = grad_cube.at[:, :, coarse_side - 1].add(
        face_high.reshape(block_count, channels, coarse_side, coarse_side)
    )
    grad_cube = grad_cube.at[:, :, 0].add(
        face_low.reshape(block_count, channels, coarse_side, coarse_side)
    )
    grad_hidden1 = grad_cube.reshape(block_count, channels, coarse_side**3)
    delta_down = (grad_hidden1 * silu_slope(coarse_pre)).astype(jnp.bfloat16)
    grad_down = jnp.einsum("bov,bkv->ok", delta_down, patches0, preferred_element_type=f32)
    down_back = jnp.einsum("ok,bov->bkv", w_down, delta_down, preferred_element_type=f32)
    grad_hidden0 = cotangent[0].astype(f32) + from_patches(down_back, coarse_side)
    delta_fine = (grad_hidden0 * silu_slope(fine_pre)).astype(jnp.bfloat16)
    delta_groups = delta_fine.reshape((block_count // 4, 4) + delta_fine.shape[1:])

    def fine_weights(total, pair):
        pad_group, delta_group = pair
        cols = lattice_columns(pad_group, EDGE)
        return (
            total + jnp.einsum("gov,gkv->ok", delta_group, cols, preferred_element_type=f32),
            None,
        )

    grad_fine, _ = lax.scan(fine_weights, jnp.zeros(w_fine.shape, f32), (pad_groups, delta_groups))
    grad_fine, grad_down, grad_coarse, grad_up = lax.psum(
        (grad_fine, grad_down, grad_coarse, grad_up), ("space", "rep")
    )
    factor = 1.0 / math.sqrt(lax.axis_size("rep") * peer_count * block_count * EDGE**3)
    return (
        decoded[None],
        grad_fine * factor,
        grad_down * factor,
        grad_coarse * factor,
        grad_up * factor,
    )


def solution(mesh):
    in_specs = (
        P("rep", "space", None, None),
        P("rep", "space", None),
        P("rep", "space", None, None),
        P(),
        P(),
        P(),
        P(),
        P("rep", "space", None, None),
    )
    out_specs = (P("rep", "space", None, None), P(), P(), P(), P())
    return jax.shard_map(shards, mesh=mesh, in_specs=in_specs, out_specs=out_specs, check_vma=False)
```

profile of v0, /device:TPU:2, one launch (start us, length us, event | category | flops | bytes accessed | tf_op | source)
XLA Modules:
  0.0 604.1 jit_solution(300199098272582646)
XLA Ops:
  8.8 1.6 gather_fusion
  10.6 3.4 collective-permute-start
  15.8 3.4 collective-permute-start.1
  43.3 2.0 concatenate.387
  48.4 3.0 copy.303
  51.4 3.8 copy.304
  55.2 1.4 maximum_bitcast_fusion.18
  58.0 2.5 pad_maximum_fusion
  80.6 1.6 gather_fusion.22
  82.1 1.6 gather_fusion.7
  83.7 1.6 gather_fusion.5
  85.3 1.6 gather_fusion.18
  86.9 1.6 gather_fusion.16
  88.4 1.6 gather_fusion.13
  90.0 1.6 gather_fusion.11
  94.1 1.7 gather_fusion.17
  105.1 3.2 fusion.228
  108.3 5.6 fusion.227
  113.9 2.1 copy.375
  116.0 2.0 copy.374
  118.0 2.0 copy.373
  120.0 2.0 copy.372
  123.0 2.1 copy.370
  125.1 2.0 copy.369
  127.1 1.3 copy.368
  129.1 1.3 copy.394
  130.4 2.0 copy.393
  133.4 2.1 copy.391
  135.5 2.0 copy.390
  137.5 2.0 copy.389
  139.5 2.0 copy.388
  141.5 2.0 copy.387
  144.6 2.1 copy.385
  146.6 2.0 copy.384
  148.6 2.0 copy.383
  150.6 2.0 copy.382
  152.7 2.0 copy.381
  158.3 1.7 constant_dynamic-update-slice_fusion.25
  160.0 1.7 constant_dynamic-update-slice_fusion.24
  161.8 1.7 constant_dynamic-update-slice_fusion.23
  180.5 4.4 multiply_convert_fusion
  189.4 2.4 collective-permute-start.2
  191.9 4.1 collective-permute-start.3
  199.2 2.1 collective-permute-done.3
  205.6 1.3 gather_fusion.55
  209.0 1.3 gather_fusion.49
  229.0 1.5 gather_fusion.31
  231.2 1.5 gather_fusion.37
  233.5 1.5 gather_fusion.54
  259.8 1.4 fusion.234
  261.2 3.1 concatenate.384
  268.8 2.0 fusion.80
  280.3 2.3 fusion.22
  283.7 2.3 fusion.27
  286.3 2.2 fusion.30
  290.6 5.0 collective-permute-start.5
  296.7 2.2 collective-permute-start.4
  300.9 6.0 collective-permute-done.4
  311.8 6.0 convolution_bitcast_fusion.2
  320.4 269.7 %all-reduce.7.cloned.1.call-done = (f32[64,1728]{1,0:T(8,128)}, f32[64,512]{1,0:T(8,128)}, f32[64,1728]{1,0:T(8,128)}, f32[64,512]{1,0:T(8,128)}) async-done(((f32[64,1728]{1,0:T(8,128)}, f32[64,512]{1,0:T(8,128)}, f32[64,1728]{1,0:T(8,128)}, f32[64,512]{1,0:T(8,128)}), (f32[64,1728]{1,0:T(8,128)}, f32[64,512]{1,0:T(8,128)}, f32[64,1728]{1,0:T(8,128)}, f32[64,512]{1,0:T(8,128)})) %all-reduce.7.cloned.1.call-update) | async-done | bytes 1146896 | tf_op jit(solution)/shard_map/psum | solution.py:216
  590.0 1.8 broadcast_multiply_fusion.1
  591.9 1.6 broadcast_multiply_fusion.3
  593.4 1.6 broadcast_multiply_fusion.2
  595.0 1.8 broadcast_multiply_fusion
  (715 shorter events, 173.2 us)
Async XLA Ops:
  7.2 257.1 %copy-start = (bf16[64,1728]{1,0:T(8,128)(2,1)S(1)}, bf16[64,1728]{1,0:T(8,128)(2,1)}, u32[]{:S(2)}) copy-start(bf16[64,1728]{1,0:T(8,128)(2,1)} %param.261) | copy-start | bytes 663556
  7.2 582.9 %all-reduce.7.cloned.1.call-start = ((), (), s32[]{:S(2)}) async-start(), calls=%async_computation | async-start | bytes 2359296 | tf_op jit(solution)/shard_map/psum | solution.py:216
  10.6 37.8 %collective-permute-start = (bf16[16,64,512]{2,1,0:T(8,128)(2,1)S(1)}, bf16[16,64,512]{2,1,0:T(8,128)(2,1)}, u32[]{:S(2)}, u32[]{:S(2)}) collective-permute-start(bf16[16,64,512]{2,1,0:T(8,128)(2,1)S(1)} %broadcast_select_fusion.1), channel_id=1, source_target_pairs={{0,2},{2,4},{4,6},{6,8},{8,10},{10,12},{12,14},{14,16},{16,18},{18... | collective-permute-start | bytes 3145736 | tf_op jit(solution)/shard_map/ppermute | solution.py:16
  15.8 35.5 %collective-permute-start.1 = (bf16[16,64,512]{2,1,0:T(8,128)(2,1)}, bf16[16,64,512]{2,1,0:T(8,128)(2,1)}, u32[]{:S(2)}, u32[]{:S(2)}) collective-permute-start(bf16[16,64,512]{2,1,0:T(8,128)(2,1)} %broadcast_select_fusion), channel_id=1, source_target_pairs={{2,0},{4,2},{6,4},{8,6},{10,8},{12,10},{14,12},{16,14},{18,16},{20... | collective-permute-start | bytes 3145736 | tf_op jit(solution)/shard_map/ppermute | solution.py:16
  19.3 22.6 %copy-start.150 = (s32[2]{0:T(128)}, s32[2]{0:T(128)S(1)}, u32[]{:S(2)}) copy-start(s32[2]{0:T(128)S(1)} %iota_multiply_fusion) | copy-start | bytes 28
  20.2 21.6 %copy-start.73 = (s32[4]{0:T(128)}, s32[4]{0:T(128)S(1)}, u32[]{:S(2)}) copy-start(s32[4]{0:T(128)S(1)} %get-tuple-element.1376) | copy-start | bytes 52
  23.2 18.7 %copy-start.43 = (s32[4]{0:T(128)}, s32[4]{0:T(128)S(1)}, u32[]{:S(2)}) copy-start(s32[4]{0:T(128)S(1)} %get-tuple-element.1356) | copy-start | bytes 52
  23.2 18.7 %copy-start.45 = (s32[4]{0:T(128)}, s32[4]{0:T(128)S(1)}, u32[]{:S(2)}) copy-start(s32[4]{0:T(128)S(1)} %get-tuple-element.1357) | copy-start | bytes 52
  23.2 18.7 %copy-start.47 = (s32[4]{0:T(128)}, s32[4]{0:T(128)S(1)}, u32[]{:S(2)}) copy-start(s32[4]{0:T(128)S(1)} %get-tuple-element.1359) | copy-start | bytes 52
  23.2 18.7 %copy-start.49 = (s32[4]{0:T(128)}, s32[4]{0:T(128)S(1)}, u32[]{:S(2)}) copy-start(s32[4]{0:T(128)S(1)} %get-tuple-element.1361) | copy-start | bytes 52
  23.2 18.7 %copy-start.107 = (s32[4]{0:T(128)}, s32[4]{0:T(128)S(1)}, u32[]{:S(2)}) copy-start(s32[4]{0:T(128)S(1)} %get-tuple-element.1352) | copy-start | bytes 52
  23.2 18.7 %copy-start.109 = (s32[4]{0:T(128)}, s32[4]{0:T(128)S(1)}, u32[]{:S(2)}) copy-start(s32[4]{0:T(128)S(1)} %get-tuple-element.1354) | copy-start | bytes 52
  23.3 18.7 %copy-start.111 = (s32[4]{0:T(128)}, s32[4]{0:T(128)S(1)}, u32[]{:S(2)}) copy-start(s32[4]{0:T(128)S(1)} %get-tuple-element.1358) | copy-start | bytes 52
  23.3 18.7 %copy-start.113 = (s32[4]{0:T(128)}, s32[4]{0:T(128)S(1)}, u32[]{:S(2)}) copy-start(s32[4]{0:T(128)S(1)} %get-tuple-element.1360) | copy-start | bytes 52
  23.3 25.0 %copy-start.51 = (s32[4]{0:T(128)}, s32[4]{0:T(128)S(1)}, u32[]{:S(2)}) copy-start(s32[4]{0:T(128)S(1)} %get-tuple-element.1362) | copy-start | bytes 52
  23.3 25.0 %copy-start.53 = (s32[4]{0:T(128)}, s32[4]{0:T(128)S(1)}, u32[]{:S(2)}) copy-start(s32[4]{0:T(128)S(1)} %get-tuple-element.1363) | copy-start | bytes 52
  23.3 25.0 %copy-start.55 = (s32[4]{0:T(128)}, s32[4]{0:T(128)S(1)}, u32[]{:S(2)}) copy-start(s32[4]{0:T(128)S(1)} %get-tuple-element.1364) | copy-start | bytes 52
  23.3 25.0 %copy-start.57 = (s32[4]{0:T(128)}, s32[4]{0:T(128)S(1)}, u32[]{:S(2)}) copy-start(s32[4]{0:T(128)S(1)} %get-tuple-element.1365) | copy-start | bytes 52
  23.3 25.0 %copy-start.59 = (s32[4]{0:T(128)}, s32[4]{0:T(128)S(1)}, u32[]{:S(2)}) copy-start(s32[4]{0:T(128)S(1)} %get-tuple-element.1366) | copy-start | bytes 52
  23.3 25.0 %copy-start.61 = (s32[4]{0:T(128)}, s32[4]{0:T(128)S(1)}, u32[]{:S(2)}) copy-start(s32[4]{0:T(128)S(1)} %get-tuple-element.1367) | copy-start | bytes 52
  23.3 25.0 %copy-start.63 = (s32[4]{0:T(128)}, s32[4]{0:T(128)S(1)}, u32[]{:S(2)}) copy-start(s32[4]{0:T(128)S(1)} %get-tuple-element.1368) | copy-start | bytes 52
  23.3 25.0 %copy-start.115 = (s32[4]{0:T(128)}, s32[4]{0:T(128)S(1)}, u32[]{:S(2)}) copy-start(s32[4]{0:T(128)S(1)} %get-tuple-element.1369) | copy-start | bytes 52
  93.1 7.8 %copy-start.140 = (pred[4]{0:T(512)(128)(4,1)S(1)}, pred[4]{0:T(512)(128)(4,1)}, u32[]{:S(2)}) copy-start(pred[4]{0:T(512)(128)(4,1)} %get-tuple-element.1560) | copy-start | bytes 16
  93.1 7.9 %copy-start.91 = (pred[4]{0:T(512)(128)(4,1)S(1)}, pred[4]{0:T(512)(128)(4,1)}, u32[]{:S(2)}) copy-start(pred[4]{0:T(512)(128)(4,1)} %get-tuple-element.1616) | copy-start | bytes 16
  93.1 7.9 %copy-start.93 = (pred[4]{0:T(512)(128)(4,1)S(1)}, pred[4]{0:T(512)(128)(4,1)}, u32[]{:S(2)}) copy-start(pred[4]{0:T(512)(128)(4,1)} %get-tuple-element.1617) | copy-start | bytes 16
  94.0 8.4 %copy-start.136 = (pred[4]{0:T(512)(128)(4,1)S(1)}, pred[4]{0:T(512)(128)(4,1)}, u32[]{:S(2)}) copy-start(pred[4]{0:T(512)(128)(4,1)} %get-tuple-element.1604) | copy-start | bytes 16
  94.1 8.4 %copy-start.137 = (pred[4]{0:T(512)(128)(4,1)S(1)}, pred[4]{0:T(512)(128)(4,1)}, u32[]{:S(2)}) copy-start(pred[4]{0:T(512)(128)(4,1)} %get-tuple-element.1605) | copy-start | bytes 16
  94.1 9.2 %copy-start.126 = (pred[4]{0:T(512)(128)(4,1)S(1)}, pred[4]{0:T(512)(128)(4,1)}, u32[]{:S(2)}) copy-start(pred[4]{0:T(512)(128)(4,1)} %get-tuple-element.1600) | copy-start | bytes 16
  94.1 9.2 %copy-start.127 = (pred[4]{0:T(512)(128)(4,1)S(1)}, pred[4]{0:T(512)(128)(4,1)}, u32[]{:S(2)}) copy-start(pred[4]{0:T(512)(128)(4,1)} %get-tuple-element.1601) | copy-start | bytes 16
  94.1 9.2 %copy-start.89 = (pred[4]{0:T(512)(128)(4,1)S(1)}, pred[4]{0:T(512)(128)(4,1)}, u32[]{:S(2)}) copy-start(pred[4]{0:T(512)(128)(4,1)} %get-tuple-element.1540) | copy-start | bytes 16
  94.1 9.2 %copy-start.90 = (pred[4]{0:T(512)(128)(4,1)S(1)}, pred[4]{0:T(512)(128)(4,1)}, u32[]{:S(2)}) copy-start(pred[4]{0:T(512)(128)(4,1)} %get-tuple-element.1541) | copy-start | bytes 16
  94.1 9.4 %copy-start.132 = (pred[4]{0:T(512)(128)(4,1)S(1)}, pred[4]{0:T(512)(128)(4,1)}, u32[]{:S(2)}) copy-start(pred[4]{0:T(512)(128)(4,1)} %get-tuple-element.1596) | copy-start | bytes 16
  94.1 9.4 %copy-start.133 = (pred[4]{0:T(512)(128)(4,1)S(1)}, pred[4]{0:T(512)(128)(4,1)}, u32[]{:S(2)}) copy-start(pred[4]{0:T(512)(128)(4,1)} %get-tuple-element.1597) | copy-start | bytes 16
  94.1 10.2 %copy-start.134 = (pred[4]{0:T(512)(128)(4,1)S(1)}, pred[4]{0:T(512)(128)(4,1)}, u32[]{:S(2)}) copy-start(pred[4]{0:T(512)(128)(4,1)} %get-tuple-element.1592) | copy-start | bytes 16
  94.1 10.2 %copy-start.135 = (pred[4]{0:T(512)(128)(4,1)S(1)}, pred[4]{0:T(512)(128)(4,1)}, u32[]{:S(2)}) copy-start(pred[4]{0:T(512)(128)(4,1)} %get-tuple-element.1593) | copy-start | bytes 16
  113.9 8.1 %copy-start.10 = (bf16[4,64,8,8,8]{1,0,4,3,2:T(4,128)(2,1)S(1)}, bf16[4,64,8,8,8]{1,0,4,3,2:T(4,128)(2,1)}, u32[]{:S(2)}) copy-start(bf16[4,64,8,8,8]{1,0,4,3,2:T(4,128)(2,1)} %get-tuple-element.1462) | copy-start | bytes 786436
  123.0 9.4 %copy-start.9 = (bf16[4,64,8,8,8]{1,0,4,3,2:T(4,128)(2,1)S(1)}, bf16[4,64,8,8,8]{1,0,4,3,2:T(4,128)(2,1)}, u32[]{:S(2)}) copy-start(bf16[4,64,8,8,8]{1,0,4,3,2:T(4,128)(2,1)} %get-tuple-element.1441) | copy-start | bytes 786436
  133.4 10.1 %copy-start.8 = (bf16[4,64,8,8,8]{1,0,4,3,2:T(4,128)(2,1)S(1)}, bf16[4,64,8,8,8]{1,0,4,3,2:T(4,128)(2,1)}, u32[]{:S(2)}) copy-start(bf16[4,64,8,8,8]{1,0,4,3,2:T(4,128)(2,1)} %get-tuple-element.1447) | copy-start | bytes 786436
  144.6 10.1 %copy-start.7 = (bf16[4,64,8,8,8]{1,0,4,3,2:T(4,128)(2,1)S(1)}, bf16[4,64,8,8,8]{1,0,4,3,2:T(4,128)(2,1)}, u32[]{:S(2)}) copy-start(bf16[4,64,8,8,8]{1,0,4,3,2:T(4,128)(2,1)} %get-tuple-element.1453) | copy-start | bytes 786436
  160.0 7.9 %copy-start.32 = (bf16[4,64,512]{2,1,0:T(8,128)(2,1)S(1)}, bf16[4,64,512]{2,1,0:T(8,128)(2,1)}, u32[]{:S(2)}) copy-start(bf16[4,64,512]{2,1,0:T(8,128)(2,1)} %copy.378) | copy-start | bytes 786436
  185.6 10.3 %copy-start.158 = (s32[5]{0:T(128)S(1)}, s32[5]{0:T(128)}, u32[]{:S(2)}) copy-start(s32[5]{0:T(128)} %concatenate.387) | copy-start | bytes 64
  185.6 10.3 %copy-start.159 = (s32[5]{0:T(128)S(1)}, s32[5]{0:T(128)}, u32[]{:S(2)}) copy-start(s32[5]{0:T(128)} %constant.3474.clone.1) | copy-start | bytes 64
  185.7 10.9 %copy-start.12 = (bf16[1,4,64,512]{3,2,1,0:T(8,128)(2,1)S(1)}, bf16[1,4,64,512]{3,2,1,0:T(8,128)(2,1)}, u32[]{:S(2)}) copy-start(bf16[1,4,64,512]{3,2,1,0:T(8,128)(2,1)} %param.263) | copy-start | bytes 786436
  187.6 10.7 %copy-start.151 = (s32[2]{0:T(128)S(1)}, s32[2]{0:T(128)}, u32[]{:S(2)}) copy-start(s32[2]{0:T(128)} %copy-done.150) | copy-start | bytes 28
  187.6 10.7 %copy-start.156 = (s32[5]{0:T(128)S(1)}, s32[5]{0:T(128)}, u32[]{:S(2)}) copy-start(s32[5]{0:T(128)} %constant.3473.clone.1) | copy-start | bytes 64
  187.6 10.7 %copy-start.157 = (s32[5]{0:T(128)S(1)}, s32[5]{0:T(128)}, u32[]{:S(2)}) copy-start(s32[5]{0:T(128)} %constant.3471.clone.1) | copy-start | bytes 64
  189.4 9.8 %collective-permute-start.2 = (bf16[16,64,64]{1,2,0:T(8,128)(2,1)S(1)}, bf16[16,64,64]{1,2,0:T(8,128)(2,1)}, u32[]{:S(2)}, u32[]{:S(2)}) collective-permute-start(bf16[16,64,64]{1,2,0:T(8,128)(2,1)S(1)} %broadcast_select_fusion.3), channel_id=1, source_target_pairs={{0,2},{2,4},{4,6},{6,8},{8,10},{10,12},{12,14},{14,16},{16,18},{18... | collective-permute-start | bytes 393224 | tf_op jit(solution)/shard_map/ppermute | solution.py:16
  191.9 9.4 %collective-permute-start.3 = (bf16[16,64,64]{1,2,0:T(8,128)(2,1)}, bf16[16,64,64]{1,2,0:T(8,128)(2,1)}, u32[]{:S(2)}, u32[]{:S(2)}) collective-permute-start(bf16[16,64,64]{1,2,0:T(8,128)(2,1)} %broadcast_select_fusion.2), channel_id=1, source_target_pairs={{2,0},{4,2},{6,4},{8,6},{10,8},{12,10},{14,12},{16,14},{18,16},{20... | collective-permute-start | bytes 393224 | tf_op jit(solution)/shard_map/ppermute | solution.py:16
  203.2 17.0 %copy-start.153 = (pred[4]{0:T(512)(128)(4,1)S(1)}, pred[4]{0:T(512)(128)(4,1)}, u32[]{:S(2)}) copy-start(pred[4]{0:T(512)(128)(4,1)} %get-tuple-element.1629) | copy-start | bytes 16
  204.7 36.3 %copy-start.122 = (pred[4]{0:T(512)(128)(4,1)S(1)}, pred[4]{0:T(512)(128)(4,1)}, u32[]{:S(2)}) copy-start(pred[4]{0:T(512)(128)(4,1)} %get-tuple-element.1572) | copy-start | bytes 16
  204.9 37.5 %copy-start.118 = (pred[4]{0:T(512)(128)(4,1)S(1)}, pred[4]{0:T(512)(128)(4,1)}, u32[]{:S(2)}) copy-start(pred[4]{0:T(512)(128)(4,1)} %get-tuple-element.1576) | copy-start | bytes 16
  205.0 37.5 %copy-start.120 = (pred[4]{0:T(512)(128)(4,1)S(1)}, pred[4]{0:T(512)(128)(4,1)}, u32[]{:S(2)}) copy-start(pred[4]{0:T(512)(128)(4,1)} %get-tuple-element.1577) | copy-start | bytes 16
  241.8 13.4 %copy-start.96 = (pred[4]{0:T(512)(128)(4,1)S(1)}, pred[4]{0:T(512)(128)(4,1)}, u32[]{:S(2)}) copy-start(pred[4]{0:T(512)(128)(4,1)} %get-tuple-element.1556) | copy-start | bytes 16
  241.8 13.4 %copy-start.98 = (pred[4]{0:T(512)(128)(4,1)S(1)}, pred[4]{0:T(512)(128)(4,1)}, u32[]{:S(2)}) copy-start(pred[4]{0:T(512)(128)(4,1)} %get-tuple-element.1557) | copy-start | bytes 16
  244.1 11.9 %copy-start.86 = (pred[4]{0:T(512)(128)(4,1)S(1)}, pred[4]{0:T(512)(128)(4,1)}, u32[]{:S(2)}) copy-start(pred[4]{0:T(512)(128)(4,1)} %get-tuple-element.1632) | copy-start | bytes 16
  244.1 11.9 %copy-start.88 = (pred[4]{0:T(512)(128)(4,1)S(1)}, pred[4]{0:T(512)(128)(4,1)}, u32[]{:S(2)}) copy-start(pred[4]{0:T(512)(128)(4,1)} %get-tuple-element.1633) | copy-start | bytes 16
  278.9 9.5 %copy-start.44 = (s32[4]{0:T(128)S(1)}, s32[4]{0:T(128)}, u32[]{:S(2)}) copy-start(s32[4]{0:T(128)} %copy-done.43) | copy-start | bytes 52
  279.8 9.4 %copy-start.110 = (s32[4]{0:T(128)S(1)}, s32[4]{0:T(128)}, u32[]{:S(2)}) copy-start(s32[4]{0:T(128)} %copy-done.109) | copy-start | bytes 52
  280.3 9.6 %copy-start.108 = (s32[4]{0:T(128)S(1)}, s32[4]{0:T(128)}, u32[]{:S(2)}) copy-start(s32[4]{0:T(128)} %copy-done.107) | copy-start | bytes 52
  289.8 9.8 %copy-start.155 = (s32[16]{0:T(128)S(1)}, s32[16]{0:T(128)}, u32[]{:S(2)}) copy-start(s32[16]{0:T(128)} %get-tuple-element.1521) | copy-start | bytes 196
  290.2 16.6 %copy-start.154 = (s32[16]{0:T(128)S(1)}, s32[16]{0:T(128)}, u32[]{:S(2)}) copy-start(s32[16]{0:T(128)} %get-tuple-element.1522) | copy-start | bytes 196
  290.6 9.0 %collective-permute-start.5 = (bf16[16,1024]{0,1:T(8,128)(2,1)S(1)}, bf16[16,1024]{0,1:T(8,128)(2,1)S(1)}, u32[]{:S(2)}, u32[]{:S(2)}) collective-permute-start(bf16[16,1024]{0,1:T(8,128)(2,1)S(1)} %bitcast.1005), channel_id=1, source_target_pairs={{0,2},{2,4},{4,6},{6,8},{8,10},{10,12},{12,14},{14,16},{16,18},{18... | collective-permute-start | bytes 98312 | tf_op jit(solution)/shard_map/ppermute | solution.py:16
  296.5 13.5 %copy-start.36 = (bf16[64,512]{1,0:T(8,128)(2,1)S(1)}, bf16[64,512]{1,0:T(8,128)(2,1)}, u32[]{:S(2)}) copy-start(bf16[64,512]{1,0:T(8,128)(2,1)} %param.260) | copy-start | bytes 196612
  296.7 10.1 %collective-permute-start.4 = (bf16[16,1024]{0,1:T(8,128)(2,1)S(1)}, bf16[16,1024]{0,1:T(8,128)(2,1)S(1)}, u32[]{:S(2)}, u32[]{:S(2)}) collective-permute-start(bf16[16,1024]{0,1:T(8,128)(2,1)S(1)} %bitcast.1004), channel_id=1, source_target_pairs={{2,0},{4,2},{6,4},{8,6},{10,8},{12,10},{14,12},{16,14},{18,16},{20... | collective-permute-start | bytes 98312 | tf_op jit(solution)/shard_map/ppermute | solution.py:16
  (103 other events, 535.4 us)
Sparse Core Ops, SparseCore 0:
  317.9 272.0 all-reduce.6
where the time goes:
time: 616 us; the launch traced here: 604 us
  waiting for transfers between devices  278 us (45%)
  local copies, waits for them, and re-layouts  182 us (30%)
  other arithmetic  74.3 us (12%)
  matrix products  31.2 us (5%)
  starting transfers between devices  20.5 us (3%)
  between operations  17.5 us (3%)
    psum x1, waiting for transfers between devices, shards(): lax.psum((grad_fine, grad_down, grad_coarse, grad_up), ('space', 'rep'))  270 us
    gather x52, local copies, waits for them, and re-layouts, assemble(): gathered = jnp.take(part_cells, jnp.maximum(source_ids, 0), axis=0)  51 us
    reshape x27, local copies, waits for them, and re-layouts, lattice_columns(): padded[:, :, a:a + side, c:c + side, e:e + side]  43.6 us
    unnamed x366, local copies, waits for them, and re-layouts  29.9 us
    ppermute x6, starting transfers between devices, passed_along(): return lax.ppermute(block, axis, route)  20.5 us
    select_n x26, other arithmetic, assemble(): jnp.where((source_ids >= 0)[:, None, None, None, None], gathered, jnp.zer...  16.6 us
    gather x27, other arithmetic  15.4 us
    dot_general x26, matrix products, shards(): jnp.einsum('bm,bcxyz->mcxyz', selector, piece, precision=lax.Precision.HI...  14.4 us
  transfers between devices with their start and end apart: 7, of which 4 were waited for; matrix products, arithmetic and copies ran while one was open for 7% of the time, Pallas kernels for 0%

commit v1 on v0

--- a/solution.py
+++ b/solution.py
@@ -213,8 +213,12 @@
         )
 
     grad_fine, _ = lax.scan(fine_weights, jnp.zeros(w_fine.shape, f32), (pad_groups, delta_groups))
-    grad_fine, grad_down, grad_coarse, grad_up = lax.psum(
-        (grad_fine, grad_down, grad_coarse, grad_up), ("space", "rep")
+
+    def _lift_seats_all(chunk):
+        return lax.psum(lax.psum(chunk, axis_name="space"), "rep")
+
+    grad_fine, grad_down, grad_coarse, grad_up = _lift_seats_all(
+        (grad_fine, grad_down, grad_coarse, grad_up)
     )
     factor = 1.0 / math.sqrt(lax.axis_size("rep") * peer_count * block_count * EDGE**3)
     return (

time: 616 us -> 610 us (level)
  the two profiles are of different devices: /device:TPU:2 before, /device:TPU:1 now
where the time goes in v1:
time: 610 us; the launch traced here: 598 us
  waiting for transfers between devices  278 us (46%)
  local copies, waits for them, and re-layouts  182 us (30%)
  other arithmetic  74.2 us (12%)
  matrix products  31.1 us (5%)
  between operations  17.4 us (3%)
  starting transfers between devices  15.3 us (3%)
    psum x2, waiting for transfers between devices, _lift_seats_all(): return lax.psum(lax.psum(chunk, axis_name='space'), 'rep')  268 us
    gather x52, local copies, waits for them, and re-layouts, assemble(): gathered = jnp.take(part_cells, jnp.maximum(source_ids, 0), axis=0)  51.1 us
    reshape x27, local copies, waits for them, and re-layouts, lattice_columns(): padded[:, :, a:a + side, c:c + side, e:e + side]  43.6 us
    unnamed x366, local copies, waits for them, and re-layouts  29.9 us
    select_n x26, other arithmetic, assemble(): jnp.where((source_ids >= 0)[:, None, None, None, None], gathered, jnp.zer...  16.5 us
    gather x27, other arithmetic  15.4 us
    ppermute x6, starting transfers between devices, passed_along(): return lax.ppermute(block, axis, route)  15.2 us
    dot_general x26, matrix products, shards(): jnp.einsum('bm,bcxyz->mcxyz', selector, piece, precision=lax.Precision.HI...  14.3 us
  transfers between devices with their start and end apart: 8, of which 5 were waited for; matrix products, arithmetic and copies ran while one was open for 7% of the time, Pallas kernels for 0%

profile of v1, /device:TPU:1, one launch (start us, length us, event | category | flops | bytes accessed | tf_op | source)
XLA Modules:
  0.0 598.2 jit_solution(11975748412356442493)
XLA Ops:
  8.8 1.6 gather_fusion
  10.6 5.0 collective-permute-start
  17.4 1.3 collective-permute-start.1
  42.6 2.0 concatenate.387
  47.7 3.0 copy.303
  50.7 3.9 copy.304
  54.6 1.4 maximum_bitcast_fusion.18
  57.3 2.5 pad_maximum_fusion
  79.9 1.6 gather_fusion.22
  81.5 1.6 gather_fusion.7
  83.1 1.6 gather_fusion.5
  84.7 1.6 gather_fusion.18
  86.2 1.6 gather_fusion.16
  87.8 1.6 gather_fusion.13
  89.4 1.6 gather_fusion.11
  93.5 1.7 gather_fusion.17
  104.6 3.2 fusion.228
  107.8 5.6 fusion.227
  113.3 2.0 copy.375
  115.4 2.0 copy.374
  117.4 2.0 copy.373
  119.4 2.0 copy.372
  122.4 2.1 copy.370
  124.5 2.0 copy.369
  126.5 1.3 copy.368
  128.5 1.3 copy.394
  129.8 2.0 copy.393
  132.8 2.1 copy.391
  134.9 2.0 copy.390
  136.9 2.0 copy.389
  138.9 2.0 copy.388
  140.9 2.0 copy.387
  144.0 2.0 copy.385
  146.0 2.0 copy.384
  148.0 2.0 copy.383
  150.0 2.0 copy.382
  152.0 2.0 copy.381
  157.7 1.7 constant_dynamic-update-slice_fusion.25
  159.4 1.7 constant_dynamic-update-slice_fusion.24
  161.1 1.7 constant_dynamic-update-slice_fusion.23
  179.9 4.4 multiply_convert_fusion
  188.8 4.7 collective-permute-start.2
  193.5 1.3 collective-permute-start.3
  198.0 4.0 collective-permute-done.3
  209.6 1.3 gather_fusion.49
  229.6 1.5 gather_fusion.31
  231.8 1.5 gather_fusion.37
  234.0 1.5 gather_fusion.54
  260.4 1.4 fusion.234
  261.8 3.1 concatenate.384
  269.3 1.9 fusion.80
  280.9 2.2 fusion.22
  284.1 2.2 fusion.27
  286.7 2.2 fusion.30
  291.0 1.5 collective-permute-start.5
  293.6 1.5 collective-permute-start.4
  297.0 5.8 collective-permute-done.4
  307.7 6.0 convolution_bitcast_fusion.2
  313.7 234.8 %all-reduce.9.cloned.1.call-done = (f32[64,1728]{1,0:T(8,128)}, f32[64,512]{1,0:T(8,128)}, f32[64,1728]{1,0:T(8,128)}, f32[64,512]{1,0:T(8,128)}) async-done(((f32[64,1728]{1,0:T(8,128)}, f32[64,512]{1,0:T(8,128)}, f32[64,1728]{1,0:T(8,128)}, f32[64,512]{1,0:T(8,128)}), (f32[64,1728]{1,0:T(8,128)}, f32[64,512]{1,0:T(8,128)}, f32[64,1728]{1,0:T(8,128)}, f32[64,512]{1,0:T(8,128)})) %all-reduce.9.cloned.1.call-update) | async-done | bytes 1146896 | tf_op jit(solution)/shard_map/psum | solution.py:218
  551.2 33.0 %all-reduce.11.cloned.1.call-done = (f32[64,1728]{1,0:T(8,128)}, f32[64,512]{1,0:T(8,128)}, f32[64,1728]{1,0:T(8,128)}, f32[64,512]{1,0:T(8,128)}) async-done(((f32[64,1728]{1,0:T(8,128)}, f32[64,512]{1,0:T(8,128)}, f32[64,1728]{1,0:T(8,128)}, f32[64,512]{1,0:T(8,128)}), (f32[64,1728]{1,0:T(8,128)}, f32[64,512]{1,0:T(8,128)}, f32[64,1728]{1,0:T(8,128)}, f32[64,512]{1,0:T(8,128)})) %all-reduce.11.cloned.1.call-update) | async-done | bytes 1146896 | tf_op jit(solution)/shard_map/psum | solution.py:218
  584.1 1.8 broadcast_multiply_fusion.1
  585.9 1.6 broadcast_multiply_fusion.3
  587.5 1.6 broadcast_multiply_fusion.2
  589.1 1.8 broadcast_multiply_fusion
  (718 shorter events, 174.2 us)
Async XLA Ops:
  7.2 257.7 %copy-start = (bf16[64,1728]{1,0:T(8,128)(2,1)S(1)}, bf16[64,1728]{1,0:T(8,128)(2,1)}, u32[]{:S(2)}) copy-start(bf16[64,1728]{1,0:T(8,128)(2,1)} %param.261) | copy-start | bytes 663556
  7.2 541.4 %all-reduce.9.cloned.1.call-start = ((), (), s32[]{:S(2)}) async-start(), calls=%async_computation | async-start | bytes 2359296 | tf_op jit(solution)/shard_map/psum | solution.py:218
  8.0 8.2 %copy-start.105 = (pred[16]{0:T(512)(128)(4,1)}, pred[16]{0:T(512)(128)(4,1)S(1)}, u32[]{:S(2)}) copy-start(pred[16]{0:T(512)(128)(4,1)S(1)} %get-tuple-element.1528) | copy-start | bytes 52
  10.6 37.1 %collective-permute-start = (bf16[16,64,512]{2,1,0:T(8,128)(2,1)S(1)}, bf16[16,64,512]{2,1,0:T(8,128)(2,1)}, u32[]{:S(2)}, u32[]{:S(2)}) collective-permute-start(bf16[16,64,512]{2,1,0:T(8,128)(2,1)S(1)} %broadcast_select_fusion.1), channel_id=1, source_target_pairs={{0,2},{2,4},{4,6},{6,8},{8,10},{10,12},{12,14},{14,16},{16,18},{18... | collective-permute-start | bytes 3145736 | tf_op jit(solution)/shard_map/ppermute | solution.py:16
  17.4 33.4 %collective-permute-start.1 = (bf16[16,64,512]{2,1,0:T(8,128)(2,1)}, bf16[16,64,512]{2,1,0:T(8,128)(2,1)}, u32[]{:S(2)}, u32[]{:S(2)}) collective-permute-start(bf16[16,64,512]{2,1,0:T(8,128)(2,1)} %broadcast_select_fusion), channel_id=1, source_target_pairs={{2,0},{4,2},{6,4},{8,6},{10,8},{12,10},{14,12},{16,14},{18,16},{20... | collective-permute-start | bytes 3145736 | tf_op jit(solution)/shard_map/ppermute | solution.py:16
  18.7 22.5 %copy-start.150 = (s32[2]{0:T(128)}, s32[2]{0:T(128)S(1)}, u32[]{:S(2)}) copy-start(s32[2]{0:T(128)S(1)} %iota_multiply_fusion) | copy-start | bytes 28
  19.6 21.6 %copy-start.73 = (s32[4]{0:T(128)}, s32[4]{0:T(128)S(1)}, u32[]{:S(2)}) copy-start(s32[4]{0:T(128)S(1)} %get-tuple-element.1376) | copy-start | bytes 52
  22.6 18.6 %copy-start.43 = (s32[4]{0:T(128)}, s32[4]{0:T(128)S(1)}, u32[]{:S(2)}) copy-start(s32[4]{0:T(128)S(1)} %get-tuple-element.1356) | copy-start | bytes 52
  22.6 18.6 %copy-start.45 = (s32[4]{0:T(128)}, s32[4]{0:T(128)S(1)}, u32[]{:S(2)}) copy-start(s32[4]{0:T(128)S(1)} %get-tuple-element.1357) | copy-start | bytes 52
  22.6 18.6 %copy-start.47 = (s32[4]{0:T(128)}, s32[4]{0:T(128)S(1)}, u32[]{:S(2)}) copy-start(s32[4]{0:T(128)S(1)} %get-tuple-element.1359) | copy-start | bytes 52
  22.6 18.6 %copy-start.49 = (s32[4]{0:T(128)}, s32[4]{0:T(128)S(1)}, u32[]{:S(2)}) copy-start(s32[4]{0:T(128)S(1)} %get-tuple-element.1361) | copy-start | bytes 52
  22.6 18.6 %copy-start.107 = (s32[4]{0:T(128)}, s32[4]{0:T(128)S(1)}, u32[]{:S(2)}) copy-start(s32[4]{0:T(128)S(1)} %get-tuple-element.1352) | copy-start | bytes 52
  22.6 18.6 %copy-start.109 = (s32[4]{0:T(128)}, s32[4]{0:T(128)S(1)}, u32[]{:S(2)}) copy-start(s32[4]{0:T(128)S(1)} %get-tuple-element.1354) | copy-start | bytes 52
  22.6 18.6 %copy-start.111 = (s32[4]{0:T(128)}, s32[4]{0:T(128)S(1)}, u32[]{:S(2)}) copy-start(s32[4]{0:T(128)S(1)} %get-tuple-element.1358) | copy-start | bytes 52
  22.7 18.6 %copy-start.113 = (s32[4]{0:T(128)}, s32[4]{0:T(128)S(1)}, u32[]{:S(2)}) copy-start(s32[4]{0:T(128)S(1)} %get-tuple-element.1360) | copy-start | bytes 52
  22.7 25.0 %copy-start.51 = (s32[4]{0:T(128)}, s32[4]{0:T(128)S(1)}, u32[]{:S(2)}) copy-start(s32[4]{0:T(128)S(1)} %get-tuple-element.1362) | copy-start | bytes 52
  22.7 25.0 %copy-start.53 = (s32[4]{0:T(128)}, s32[4]{0:T(128)S(1)}, u32[]{:S(2)}) copy-start(s32[4]{0:T(128)S(1)} %get-tuple-element.1363) | copy-start | bytes 52
  22.7 25.0 %copy-start.55 = (s32[4]{0:T(128)}, s32[4]{0:T(128)S(1)}, u32[]{:S(2)}) copy-start(s32[4]{0:T(128)S(1)} %get-tuple-element.1364) | copy-start | bytes 52
  22.7 25.0 %copy-start.57 = (s32[4]{0:T(128)}, s32[4]{0:T(128)S(1)}, u32[]{:S(2)}) copy-start(s32[4]{0:T(128)S(1)} %get-tuple-element.1365) | copy-start | bytes 52
  22.7 25.0 %copy-start.59 = (s32[4]{0:T(128)}, s32[4]{0:T(128)S(1)}, u32[]{:S(2)}) copy-start(s32[4]{0:T(128)S(1)} %get-tuple-element.1366) | copy-start | bytes 52
  22.7 25.0 %copy-start.61 = (s32[4]{0:T(128)}, s32[4]{0:T(128)S(1)}, u32[]{:S(2)}) copy-start(s32[4]{0:T(128)S(1)} %get-tuple-element.1367) | copy-start | bytes 52
  22.7 25.0 %copy-start.63 = (s32[4]{0:T(128)}, s32[4]{0:T(128)S(1)}, u32[]{:S(2)}) copy-start(s32[4]{0:T(128)S(1)} %get-tuple-element.1368) | copy-start | bytes 52
  22.7 25.0 %copy-start.115 = (s32[4]{0:T(128)}, s32[4]{0:T(128)S(1)}, u32[]{:S(2)}) copy-start(s32[4]{0:T(128)S(1)} %get-tuple-element.1369) | copy-start | bytes 52
  92.5 8.0 %copy-start.91 = (pred[4]{0:T(512)(128)(4,1)S(1)}, pred[4]{0:T(512)(128)(4,1)}, u32[]{:S(2)}) copy-start(pred[4]{0:T(512)(128)(4,1)} %get-tuple-element.1620) | copy-start | bytes 16
  92.5 8.0 %copy-start.93 = (pred[4]{0:T(512)(128)(4,1)S(1)}, pred[4]{0:T(512)(128)(4,1)}, u32[]{:S(2)}) copy-start(pred[4]{0:T(512)(128)(4,1)} %get-tuple-element.1621) | copy-start | bytes 16
  93.4 8.4 %copy-start.136 = (pred[4]{0:T(512)(128)(4,1)S(1)}, pred[4]{0:T(512)(128)(4,1)}, u32[]{:S(2)}) copy-start(pred[4]{0:T(512)(128)(4,1)} %get-tuple-element.1608) | copy-start | bytes 16
  93.4 8.4 %copy-start.137 = (pred[4]{0:T(512)(128)(4,1)S(1)}, pred[4]{0:T(512)(128)(4,1)}, u32[]{:S(2)}) copy-start(pred[4]{0:T(512)(128)(4,1)} %get-tuple-element.1609) | copy-start | bytes 16
  93.4 9.2 %copy-start.126 = (pred[4]{0:T(512)(128)(4,1)S(1)}, pred[4]{0:T(512)(128)(4,1)}, u32[]{:S(2)}) copy-start(pred[4]{0:T(512)(128)(4,1)} %get-tuple-element.1604) | copy-start | bytes 16
  93.4 9.2 %copy-start.127 = (pred[4]{0:T(512)(128)(4,1)S(1)}, pred[4]{0:T(512)(128)(4,1)}, u32[]{:S(2)}) copy-start(pred[4]{0:T(512)(128)(4,1)} %get-tuple-element.1605) | copy-start | bytes 16
  93.5 9.3 %copy-start.89 = (pred[4]{0:T(512)(128)(4,1)S(1)}, pred[4]{0:T(512)(128)(4,1)}, u32[]{:S(2)}) copy-start(pred[4]{0:T(512)(128)(4,1)} %get-tuple-element.1544) | copy-start | bytes 16
  93.5 9.3 %copy-start.90 = (pred[4]{0:T(512)(128)(4,1)S(1)}, pred[4]{0:T(512)(128)(4,1)}, u32[]{:S(2)}) copy-start(pred[4]{0:T(512)(128)(4,1)} %get-tuple-element.1545) | copy-start | bytes 16
  93.5 9.4 %copy-start.132 = (pred[4]{0:T(512)(128)(4,1)S(1)}, pred[4]{0:T(512)(128)(4,1)}, u32[]{:S(2)}) copy-start(pred[4]{0:T(512)(128)(4,1)} %get-tuple-element.1600) | copy-start | bytes 16
  93.5 9.4 %copy-start.133 = (pred[4]{0:T(512)(128)(4,1)S(1)}, pred[4]{0:T(512)(128)(4,1)}, u32[]{:S(2)}) copy-start(pred[4]{0:T(512)(128)(4,1)} %get-tuple-element.1601) | copy-start | bytes 16
  93.5 10.3 %copy-start.134 = (pred[4]{0:T(512)(128)(4,1)S(1)}, pred[4]{0:T(512)(128)(4,1)}, u32[]{:S(2)}) copy-start(pred[4]{0:T(512)(128)(4,1)} %get-tuple-element.1596) | copy-start | bytes 16
  93.5 10.3 %copy-start.135 = (pred[4]{0:T(512)(128)(4,1)S(1)}, pred[4]{0:T(512)(128)(4,1)}, u32[]{:S(2)}) copy-start(pred[4]{0:T(512)(128)(4,1)} %get-tuple-element.1597) | copy-start | bytes 16
  113.3 8.1 %copy-start.10 = (bf16[4,64,8,8,8]{1,0,4,3,2:T(4,128)(2,1)S(1)}, bf16[4,64,8,8,8]{1,0,4,3,2:T(4,128)(2,1)}, u32[]{:S(2)}) copy-start(bf16[4,64,8,8,8]{1,0,4,3,2:T(4,128)(2,1)} %get-tuple-element.1466) | copy-start | bytes 786436
  122.4 9.4 %copy-start.9 = (bf16[4,64,8,8,8]{1,0,4,3,2:T(4,128)(2,1)S(1)}, bf16[4,64,8,8,8]{1,0,4,3,2:T(4,128)(2,1)}, u32[]{:S(2)}) copy-start(bf16[4,64,8,8,8]{1,0,4,3,2:T(4,128)(2,1)} %get-tuple-element.1445) | copy-start | bytes 786436
  132.8 10.1 %copy-start.8 = (bf16[4,64,8,8,8]{1,0,4,3,2:T(4,128)(2,1)S(1)}, bf16[4,64,8,8,8]{1,0,4,3,2:T(4,128)(2,1)}, u32[]{:S(2)}) copy-start(bf16[4,64,8,8,8]{1,0,4,3,2:T(4,128)(2,1)} %get-tuple-element.1451) | copy-start | bytes 786436
  144.0 10.1 %copy-start.7 = (bf16[4,64,8,8,8]{1,0,4,3,2:T(4,128)(2,1)S(1)}, bf16[4,64,8,8,8]{1,0,4,3,2:T(4,128)(2,1)}, u32[]{:S(2)}) copy-start(bf16[4,64,8,8,8]{1,0,4,3,2:T(4,128)(2,1)} %get-tuple-element.1457) | copy-start | bytes 786436
  185.0 9.8 %copy-start.158 = (s32[5]{0:T(128)S(1)}, s32[5]{0:T(128)}, u32[]{:S(2)}) copy-start(s32[5]{0:T(128)} %concatenate.387) | copy-start | bytes 64
  185.1 9.8 %copy-start.159 = (s32[5]{0:T(128)S(1)}, s32[5]{0:T(128)}, u32[]{:S(2)}) copy-start(s32[5]{0:T(128)} %constant.3474.clone.1) | copy-start | bytes 64
  185.1 10.4 %copy-start.12 = (bf16[1,4,64,512]{3,2,1,0:T(8,128)(2,1)S(1)}, bf16[1,4,64,512]{3,2,1,0:T(8,128)(2,1)}, u32[]{:S(2)}) copy-start(bf16[1,4,64,512]{3,2,1,0:T(8,128)(2,1)} %param.263) | copy-start | bytes 786436
  187.0 10.2 %copy-start.151 = (s32[2]{0:T(128)S(1)}, s32[2]{0:T(128)}, u32[]{:S(2)}) copy-start(s32[2]{0:T(128)} %copy-done.150) | copy-start | bytes 28
  187.0 10.2 %copy-start.156 = (s32[5]{0:T(128)S(1)}, s32[5]{0:T(128)}, u32[]{:S(2)}) copy-start(s32[5]{0:T(128)} %constant.3473.clone.1) | copy-start | bytes 64
  187.0 10.2 %copy-start.157 = (s32[5]{0:T(128)S(1)}, s32[5]{0:T(128)}, u32[]{:S(2)}) copy-start(s32[5]{0:T(128)} %constant.3471.clone.1) | copy-start | bytes 64
  188.8 9.2 %collective-permute-start.2 = (bf16[16,64,64]{1,2,0:T(8,128)(2,1)S(1)}, bf16[16,64,64]{1,2,0:T(8,128)(2,1)}, u32[]{:S(2)}, u32[]{:S(2)}) collective-permute-start(bf16[16,64,64]{1,2,0:T(8,128)(2,1)S(1)} %broadcast_select_fusion.3), channel_id=1, source_target_pairs={{0,2},{2,4},{4,6},{6,8},{8,10},{10,12},{12,14},{14,16},{16,18},{18... | collective-permute-start | bytes 393224 | tf_op jit(solution)/shard_map/ppermute | solution.py:16
  193.5 8.5 %collective-permute-start.3 = (bf16[16,64,64]{1,2,0:T(8,128)(2,1)}, bf16[16,64,64]{1,2,0:T(8,128)(2,1)}, u32[]{:S(2)}, u32[]{:S(2)}) collective-permute-start(bf16[16,64,64]{1,2,0:T(8,128)(2,1)} %broadcast_select_fusion.2), channel_id=1, source_target_pairs={{2,0},{4,2},{6,4},{8,6},{10,8},{12,10},{14,12},{16,14},{18,16},{20... | collective-permute-start | bytes 393224 | tf_op jit(solution)/shard_map/ppermute | solution.py:16
  203.9 16.9 %copy-start.153 = (pred[4]{0:T(512)(128)(4,1)S(1)}, pred[4]{0:T(512)(128)(4,1)}, u32[]{:S(2)}) copy-start(pred[4]{0:T(512)(128)(4,1)} %get-tuple-element.1633) | copy-start | bytes 16
  205.4 36.2 %copy-start.122 = (pred[4]{0:T(512)(128)(4,1)S(1)}, pred[4]{0:T(512)(128)(4,1)}, u32[]{:S(2)}) copy-start(pred[4]{0:T(512)(128)(4,1)} %get-tuple-element.1576) | copy-start | bytes 16
  205.7 37.4 %copy-start.118 = (pred[4]{0:T(512)(128)(4,1)S(1)}, pred[4]{0:T(512)(128)(4,1)}, u32[]{:S(2)}) copy-start(pred[4]{0:T(512)(128)(4,1)} %get-tuple-element.1580) | copy-start | bytes 16
  205.7 37.4 %copy-start.120 = (pred[4]{0:T(512)(128)(4,1)S(1)}, pred[4]{0:T(512)(128)(4,1)}, u32[]{:S(2)}) copy-start(pred[4]{0:T(512)(128)(4,1)} %get-tuple-element.1581) | copy-start | bytes 16
  242.3 13.4 %copy-start.96 = (pred[4]{0:T(512)(128)(4,1)S(1)}, pred[4]{0:T(512)(128)(4,1)}, u32[]{:S(2)}) copy-start(pred[4]{0:T(512)(128)(4,1)} %get-tuple-element.1560) | copy-start | bytes 16
  242.3 13.4 %copy-start.98 = (pred[4]{0:T(512)(128)(4,1)S(1)}, pred[4]{0:T(512)(128)(4,1)}, u32[]{:S(2)}) copy-start(pred[4]{0:T(512)(128)(4,1)} %get-tuple-element.1561) | copy-start | bytes 16
  244.7 11.9 %copy-start.86 = (pred[4]{0:T(512)(128)(4,1)S(1)}, pred[4]{0:T(512)(128)(4,1)}, u32[]{:S(2)}) copy-start(pred[4]{0:T(512)(128)(4,1)} %get-tuple-element.1636) | copy-start | bytes 16
  244.7 11.9 %copy-start.88 = (pred[4]{0:T(512)(128)(4,1)S(1)}, pred[4]{0:T(512)(128)(4,1)}, u32[]{:S(2)}) copy-start(pred[4]{0:T(512)(128)(4,1)} %get-tuple-element.1637) | copy-start | bytes 16
  279.5 9.4 %copy-start.44 = (s32[4]{0:T(128)S(1)}, s32[4]{0:T(128)}, u32[]{:S(2)}) copy-start(s32[4]{0:T(128)} %copy-done.43) | copy-start | bytes 52
  280.3 9.3 %copy-start.110 = (s32[4]{0:T(128)S(1)}, s32[4]{0:T(128)}, u32[]{:S(2)}) copy-start(s32[4]{0:T(128)} %copy-done.109) | copy-start | bytes 52
  280.8 9.4 %copy-start.108 = (s32[4]{0:T(128)S(1)}, s32[4]{0:T(128)}, u32[]{:S(2)}) copy-start(s32[4]{0:T(128)} %copy-done.107) | copy-start | bytes 52
  290.6 12.2 %copy-start.154 = (s32[16]{0:T(128)S(1)}, s32[16]{0:T(128)}, u32[]{:S(2)}) copy-start(s32[16]{0:T(128)} %get-tuple-element.1526) | copy-start | bytes 196
  291.0 4.8 collective-permute-start.5
  293.4 12.5 %copy-start.36 = (bf16[64,512]{1,0:T(8,128)(2,1)S(1)}, bf16[64,512]{1,0:T(8,128)(2,1)}, u32[]{:S(2)}) copy-start(bf16[64,512]{1,0:T(8,128)(2,1)} %param.260) | copy-start | bytes 196612
  293.6 9.1 %collective-permute-start.4 = (bf16[16,1024]{0,1:T(8,128)(2,1)S(1)}, bf16[16,1024]{0,1:T(8,128)(2,1)S(1)}, u32[]{:S(2)}, u32[]{:S(2)}) collective-permute-start(bf16[16,1024]{0,1:T(8,128)(2,1)S(1)} %bitcast.1004), channel_id=1, source_target_pairs={{2,0},{4,2},{6,4},{8,6},{10,8},{12,10},{14,12},{16,14},{18,16},{20... | collective-permute-start | bytes 98312 | tf_op jit(solution)/shard_map/ppermute | solution.py:16
  313.6 234.9 %copy-start.37 = (bf16[64,512]{1,0:T(8,128)(2,1)S(1)}, bf16[64,512]{1,0:T(8,128)(2,1)}, u32[]{:S(2)}) copy-start(bf16[64,512]{1,0:T(8,128)(2,1)} %param.262) | copy-start | bytes 196612
  313.7 270.5 %all-reduce.11.cloned.1.call-start = ((), (), s32[]{:S(2)}) async-start(), calls=%async_computation.1 | async-start | bytes 2359296 | tf_op jit(solution)/shard_map/psum | solution.py:218
  (104 other events, 544.2 us)
Sparse Core Ops, SparseCore 0:
  313.8 234.7 all-reduce.8
  551.4 32.7 all-reduce.10
